TPU v7x, 256 devices: a whole 4x4x8 slice. The times are simulated.
256 devices in a mesh: row: 16 (over x_lo, y, core), col: 16 (over x_hi, z).
Axes of the slice: x: 4 (x_hi: 2, x_lo: 2; x = x_hi * 2 + x_lo), y: 4, z: 8, core: 2. Of those that a mesh axis runs over, the one named last changes fastest.
Arguments:
- top_inverse: bfloat16 [16, 16, 16, 16, 128, 128], P('row', None, None, 'col'), as said below
- upper_panel: bfloat16 [3, 16, 16, 128, 128], P(None, 'row', 'col'), may hold values from -0.25 to 0.25
- upper_pattern: int32 [3, 16, 16], P(None, 'row', 'col'), may hold values from 0 to 1
- upper_diagonal: float32 [3, 128, 128], replicated, may hold values from -6 to 6
- lower_panel: bfloat16 [8, 16, 16, 128, 128], P(None, 'row', 'col'), may hold values from -0.25 to 0.25
- lower_pattern: int32 [8, 16, 16], P(None, 'row', 'col'), may hold values from 0 to 1, as said below
- parents: int32 [8], replicated, may hold values from 0 to 2, as said below
- parent_panel: bfloat16 [8, 128, 128], replicated, may hold values from -0.5 to 0.5
- lower_diagonal: float32 [8, 128, 128], replicated, may hold values from -6 to 6
Outputs:
- upper_columns: bfloat16 [3, 16, 16, 128, 128], P(None, 'row', 'col')
- upper_blocks: float32 [3, 128, 128], replicated
- lower_columns: bfloat16 [8, 16, 16, 128, 128], P(None, 'row', 'col')
- lower_cross: float32 [8, 128, 128], replicated
- lower_blocks: float32 [8, 128, 128], replicated
Inputs may be any that keep to these rules, and one draw needn't show every extreme that they name: top_inverse is symmetric: block (I, J) is the transpose of block (J, I). `lower_pattern`: A second-level pattern is zero wherever the pattern of its parent is zero. `parents`: every first-level supernode is the parent of some second-level supernode.
All inputs are finite; a program needn't handle non-finite values.
Results may differ from a plain program's by a relative error of at most 0.0041.
Values may be sent and summed in bfloat16 or wider, within the bound.
A program may use at most 128 MiB of HBM per device.

v0:
```python
import jax
import jax.numpy as jnp
from jax import lax
from jax.sharding import PartitionSpec as P

HIGH = lax.Precision.HIGHEST


def by_rows(top_inverse, panel):
    partial_value = jnp.einsum(
        "aibjxy,kbjyz->iakxz",
        top_inverse,
        lax.all_gather(panel, "row", axis=1, tiled=True),
        preferred_element_type=jnp.float32,
    )
    reduced = lax.psum_scatter(partial_value, "col", scatter_dimension=0, tiled=True)
    return jnp.transpose(reduced, (2, 1, 0, 3, 4))


def upper_part(upper_product, upper_mask, upper_masked, lower_masked, parents):
    upper_columns = (-upper_product * upper_mask).astype(jnp.bfloat16)
    selected = jnp.take(upper_columns, parents, axis=0)
    local_upper = jnp.einsum(
        "ktsxy,ktsxz->kyz", upper_masked, upper_columns, preferred_element_type=jnp.float32
    )
    local_cross = jnp.einsum(
        "mtsxy,mtsxz->myz", selected, lower_masked, preferred_element_type=jnp.float32
    )
    return (upper_columns, selected, local_upper, local_cross)


def lower_part(lower_product, selected, parent_panel, lower_mask, lower_masked):
    extension = jnp.einsum(
        "mtsxy,myz->mtsxz", selected, parent_panel, preferred_element_type=jnp.float32
    )
    lower_columns = (-(lower_product + extension) * lower_mask).astype(jnp.bfloat16)
    local_lower = jnp.einsum(
        "mtsxy,mtsxz->myz", lower_masked, lower_columns, preferred_element_type=jnp.float32
    )
    return (lower_columns, local_lower)


def per_device(
    top_inverse,
    upper_panel,
    upper_pattern,
    upper_diagonal,
    lower_panel,
    lower_pattern,
    parents,
    parent_panel,
    lower_diagonal,
):
    upper_mask = upper_pattern.astype(jnp.float32)[:, :, :, None, None]
    upper_masked = upper_panel * upper_mask.astype(jnp.bfloat16)
    lower_mask = lower_pattern.astype(jnp.float32)[:, :, :, None, None]
    lower_masked = lower_panel * lower_mask.astype(jnp.bfloat16)
    upper_product = by_rows(top_inverse, upper_masked)
    upper_columns, selected, local_upper, local_cross = upper_part(
        upper_product, upper_mask, upper_masked, lower_masked, parents
    )
    summed_upper, summed_cross = lax.psum((local_upper, local_cross), ("row", "col"))
    lower_product = by_rows(top_inverse, lower_masked)
    lower_columns, local_lower = lower_part(
        lower_product, selected, parent_panel, lower_mask, lower_masked
    )
    summed_lower = lax.psum(local_lower, ("row", "col"))
    upper_blocks = upper_diagonal - summed_upper
    panel_wide = parent_panel.astype(jnp.float32)
    parent_blocks = jnp.take(upper_blocks, parents, axis=0)
    lower_cross = -summed_cross - jnp.einsum(
        "mxy,myz->mxz", parent_blocks, panel_wide, precision=HIGH
    )
    lower_blocks = (
        lower_diagonal
        - summed_lower
        - jnp.einsum("myx,myz->mxz", panel_wide, lower_cross, precision=HIGH)
    )
    return (upper_columns, upper_blocks, lower_columns, lower_cross, lower_blocks)


def solution(mesh):
    return jax.shard_map(
        per_device,
        mesh=mesh,
        in_specs=(
            P("row", None, None, "col", None, None),
            P(None, "row", "col", None, None),
            P(None, "row", "col"),
            P(),
            P(None, "row", "col", None, None),
            P(None, "row", "col"),
            P(),
            P(),
            P(),
        ),
        out_specs=(
            P(None, "row", "col", None, None),
            P(),
            P(None, "row", "col", None, None),
            P(),
            P(),
        ),
        check_vma=False,
    )
```

profile of v0, /device:TPU:8, one launch (start us, length us, event | category | flops | bytes accessed | tf_op | source)
XLA Modules:
  0.0 649.7 jit_solution(10669901075646859960)
XLA Ops:
  7.2 0.0 copy-start
  7.2 0.0 all-gather.3.cloned.1.call-start
  7.2 0.7 fusion.31
  7.9 1.0 copy.49
  8.9 0.7 broadcast_multiply_fusion.1
  9.7 0.0 all-gather.3.cloned.1.call-update
  9.7 0.0 all-gather.5.cloned.1.call-start
  9.7 1.1 copy.51
  10.9 0.7 convert_bitcast_fusion
  11.5 0.8 broadcast_multiply_fusion
  12.3 0.0 all-gather.5.cloned.1.call-update
  12.3 0.0 all-reduce.9.cloned.1.call-start
  12.4 36.1 %all-gather.3.cloned.1.call-done = bf16[3,16,1,128,128]{3,4,1,0,2:T(8,128)(2,1)} async-done(((bf16[3,1,1,128,128]{3,4,1,0,2:T(8,128)(2,1)}), bf16[3,16,1,128,128]{3,4,1,0,2:T(8,128)(2,1)}) %all-gather.3.cloned.1.call-update) | async-done | bytes 1572880 | tf_op jit(solution)/shard_map/all_gather | solution.py:13
  48.5 7.5 %fusion.10 = f32[16,1,3,128,128]{3,4,0,2,1:T(8,128)} fusion(bf16[1,16,16,1,128,128]{5,4,3,2,1,0:T(8,128)(2,1)} %param.9, bf16[3,16,1,128,128]{3,4,1,0,2:T(8,128)(2,1)} %all-gather.3.cloned.1.call-done), kind=kOutput, calls=%fused_computation.8 | convolution fusion | flops 3221225472 | bytes 13107200 | tf_op jit(solution)/shard_map/aibjxy,kbjyz->iakxz/dot_general | solution.py:10
  55.9 34.7 %all-gather.5.cloned.1.call-done = bf16[8,16,1,128,128]{3,4,1,0,2:T(8,128)(2,1)} async-done(((bf16[8,1,1,128,128]{3,4,1,0,2:T(8,128)(2,1)}), bf16[8,16,1,128,128]{3,4,1,0,2:T(8,128)(2,1)}) %all-gather.5.cloned.1.call-update) | async-done | bytes 4194320 | tf_op jit(solution)/shard_map/all_gather | solution.py:13
  90.6 13.6 %fusion.5 = f32[16,1,8,128,128]{3,4,0,2,1:T(8,128)} fusion(bf16[1,16,16,1,128,128]{5,4,3,2,1,0:T(8,128)(2,1)} %param.9, bf16[8,16,1,128,128]{3,4,1,0,2:T(8,128)(2,1)} %all-gather.5.cloned.1.call-done), kind=kOutput, calls=%fused_computation.7 | convolution fusion | flops 8589934592 | bytes 20971520 | tf_op jit(solution)/shard_map/aibjxy,kbjyz->iakxz/dot_general | solution.py:10
  104.2 0.0 all-reduce.9.cloned.1.call-update
  104.3 0.0 copy-start.1
  104.3 0.0 all-reduce.7.cloned.1.call-start
  104.3 0.6 copy-done.9
  104.9 0.6 dynamic-slice
  105.5 0.0 copy-done.8
  105.5 264.7 %all-reduce.9.cloned.1.call-done = (f32[16,1,3,128,128]{3,4,0,2,1:T(8,128)}, f32[16,1,8,128,128]{3,4,0,2,1:T(8,128)}) async-done(((f32[16,1,3,128,128]{3,4,0,2,1:T(8,128)}, f32[16,1,8,128,128]{3,4,0,2,1:T(8,128)}), (f32[16,1,3,128,128]{3,4,0,2,1:T(8,128)}, f32[16,1,8,128,128]{3,4,0,2,1:T(8,128)})) %all-reduce.9.cloned.1.call-update) | async-done | bytes 11534352
  370.2 1.6 constant_dynamic-slice_fusion.1
  371.8 0.0 copy-start.7
  371.8 0.1 copy.50
  371.9 0.7 fusion.37
  372.7 0.0 copy-done.5
  372.7 0.9 fusion.27
  373.6 1.7 constant_dynamic-slice_fusion
  375.3 0.2 copy.52
  375.5 0.6 gather_fusion
  376.1 0.0 copy-done.1
  376.2 0.0 copy-start.6
  376.2 1.2 fusion.21
  377.4 0.3 fusion.17
  377.7 0.0 copy-start.4
  377.7 1.0 fusion.19
  378.7 0.0 all-reduce.7.cloned.1.call-update
  378.7 258.8 %all-reduce.7.cloned.1.call-done = (f32[3,128,128]{2,1,0:T(8,128)}, f32[8,128,128]{2,1,0:T(8,128)}, f32[8,128,128]{2,1,0:T(8,128)}) async-done(((f32[3,128,128]{2,1,0:T(8,128)}, f32[8,128,128]{2,1,0:T(8,128)}, f32[8,128,128]{2,1,0:T(8,128)}), (f32[3,128,128]{2,1,0:T(8,128)}, f32[8,128,128]{2,1,0:T(8,128)}, f32[8,128,128]{2,1,0:T(8,128)})) %all-reduce.7.cloned.1.call-update) | async-done | bytes 1245200 | tf_op jit(solution)/shard_map/psum | solution.py:62
  637.5 0.9 sub.12
  638.5 0.0 copy-start.2
  638.5 0.6 gather_fusion.1
  639.1 1.5 convolution_subtract_fusion
  640.6 0.0 copy-start.3
  640.6 0.0 copy-done.6
  640.6 2.5 fusion.16
  643.1 0.0 copy-done.2
  (10 shorter events, 0.0 us)
Async XLA Ops:
  7.2 370.2 %copy-start = (bf16[8,128,128]{2,1,0:T(8,128)(2,1)S(1)}, bf16[8,128,128]{2,1,0:T(8,128)(2,1)}, u32[]{:S(2)}) copy-start(bf16[8,128,128]{2,1,0:T(8,128)(2,1)} %param.16) | copy-start | bytes 786436
  7.2 41.3 %all-gather.3.cloned.1.call-start = ((), (), s32[]{:S(2)}) async-start(), calls=%async_computation | async-start | bytes 1671168 | tf_op jit(solution)/shard_map/all_gather | solution.py:13
  9.7 80.9 %all-gather.5.cloned.1.call-start = ((), (), s32[]{:S(2)}) async-start(), calls=%async_computation.1 | async-start | bytes 4456448 | tf_op jit(solution)/shard_map/all_gather | solution.py:13
  12.3 357.9 %all-reduce.9.cloned.1.call-start = ((), (), s32[]{:S(2)}) async-start(), calls=%async_computation.3 | async-start | bytes 23068672
  104.2 0.7 copy-start.9
  104.2 1.3 copy-start.8
  104.2 268.5 %copy-start.5 = (bf16[3,1,1,128,128]{3,4,1,0,2:T(8,128)(2,1)S(1)}, bf16[3,1,1,128,128]{3,4,1,0,2:T(8,128)(2,1)}, u32[]{:S(2)}) copy-start(bf16[3,1,1,128,128]{3,4,1,0,2:T(8,128)(2,1)} %broadcast_multiply_fusion.1) | copy-start | bytes 294916
  104.3 271.9 %copy-start.1 = (bf16[8,1,1,128,128]{3,4,1,0,2:T(8,128)(2,1)S(1)}, bf16[8,1,1,128,128]{3,4,1,0,2:T(8,128)(2,1)}, u32[]{:S(2)}) copy-start(bf16[8,1,1,128,128]{3,4,1,0,2:T(8,128)(2,1)} %broadcast_multiply_fusion) | copy-start | bytes 786436
  104.3 533.2 %all-reduce.7.cloned.1.call-start = ((), (), s32[]{:S(2)}) async-start(), calls=%async_computation.2 | async-start | bytes 2490368 | tf_op jit(solution)/shard_map/psum | solution.py:62
  371.8 265.7 %copy-start.7 = (f32[3,128,128]{2,1,0:T(8,128)S(1)}, f32[3,128,128]{2,1,0:T(8,128)}, u32[]{:S(2)}) copy-start(f32[3,128,128]{2,1,0:T(8,128)} %param.12) | copy-start | bytes 589828
  376.2 264.4 %copy-start.6 = (f32[8,128,128]{2,1,0:T(8,128)S(1)}, f32[8,128,128]{2,1,0:T(8,128)}, u32[]{:S(2)}) copy-start(f32[8,128,128]{2,1,0:T(8,128)} %param.17) | copy-start | bytes 1572868
  377.7 265.4 %copy-start.4 = (bf16[8,128,128]{2,1,0:T(8,128)(2,1)}, bf16[8,128,128]{2,1,0:T(8,128)(2,1)S(1)}, u32[]{:S(2)}) copy-start(bf16[8,128,128]{2,1,0:T(8,128)(2,1)S(1)} %fusion.17) | copy-start | bytes 786436
  638.5 4.6 copy-start.2
  640.6 2.5 copy-start.3
Sparse Core Ops, SparseCore 0:
  10.4 38.0 all-gather.2
  50.8 39.7 all-gather.4
  104.4 265.7 all-reduce.8
  378.9 258.6 all-reduce.6
where the time goes:
time: 650 us
  waiting for transfers between devices  594 us (91%)
  matrix products  28.5 us (4%)
  between operations  13.9 us (2%)
  local copies, waits for them, and re-layouts  8.16 us (1%)
    unnamed x5, waiting for transfers between devices  265 us
    psum x1, waiting for transfers between devices, per_device(): lax.psum((local_upper, local_cross), ('row', 'col'))  259 us
    all_gather x2, waiting for transfers between devices, by_rows(): lax.all_gather(panel, 'row', axis=1, tiled=True)  70.7 us
    dot_general x2, matrix products, by_rows(): jnp.einsum('aibjxy,kbjyz->iakxz', top_inverse, lax.all_gather(panel, 'row...  21.1 us
  transfers between devices with their start and end apart: 4, of which 4 were waited for; matrix products, arithmetic and copies ran while one was open for 2% of the time, Pallas kernels for 0%

commit v1 on v0

--- a/solution.py
+++ b/solution.py
@@ -4,6 +4,11 @@
 from jax.sharding import PartitionSpec as P
 
 HIGH = lax.Precision.HIGHEST
+
+
+def axis_by_axis(array, inner_axis, outer_axis):
+    partial = lax.psum(array, inner_axis)
+    return lax.psum(partial, outer_axis)
 
 
 def by_rows(top_inverse, panel):
@@ -59,7 +64,7 @@
     upper_columns, selected, local_upper, local_cross = upper_part(
         upper_product, upper_mask, upper_masked, lower_masked, parents
     )
-    summed_upper, summed_cross = lax.psum((local_upper, local_cross), ("row", "col"))
+    summed_upper, summed_cross = axis_by_axis((local_upper, local_cross), "row", "col")
     lower_product = by_rows(top_inverse, lower_masked)
     lower_columns, local_lower = lower_part(
         lower_product, selected, parent_panel, lower_mask, lower_masked

time: 650 us -> 880 us (1.35)
  waiting for transfers between devices: 594 us -> 825 us
    psum x1 -> x3, waiting for transfers between devices: 259 us -> 587 us  [the longest x1 251 us: per_device(): summed_lower = lax.psum(local_lower, ('row', 'col'))]
    unnamed x5 -> x7, waiting for transfers between devices: 265 us -> 167 us
  transfers between devices with their start and end apart: 4 -> 6, of which waited for: 4 -> 6; matrix products, arithmetic and copies ran while one was open for 2% -> 3% of each run, Pallas kernels for 0% -> 0%
where the time goes in v1:
time: 880 us
  waiting for transfers between devices  825 us (94%)
  matrix products  29.3 us (3%)
  between operations  14.3 us (2%)
    psum x1, waiting for transfers between devices, per_device(): summed_lower = lax.psum(local_lower, ('row', 'col'))  251 us
    psum x1, waiting for transfers between devices, axis_by_axis(): return lax.psum(partial, outer_axis)  225 us
    unnamed x7, waiting for transfers between devices  167 us
    psum x1, waiting for transfers between devices, axis_by_axis(): partial = lax.psum(array, inner_axis)  111 us
    all_gather x2, waiting for transfers between devices, by_rows(): lax.all_gather(panel, 'row', axis=1, tiled=True)  71 us
    dot_general x2, matrix products, by_rows(): jnp.einsum('aibjxy,kbjyz->iakxz', top_inverse, lax.all_gather(panel, 'row...  21.1 us
  transfers between devices with their start and end apart: 6, of which 6 were waited for; matrix products, arithmetic and copies ran while one was open for 3% of the time, Pallas kernels for 0%

profile of v1, /device:TPU:8, one launch (start us, length us, event | category | flops | bytes accessed | tf_op | source)
XLA Modules:
  0.0 879.6 jit_solution(14832193262104455089)
XLA Ops:
  7.2 0.0 copy-start
  7.2 0.0 all-gather.3.cloned.1.call-start
  7.2 0.7 fusion.31
  7.9 1.0 copy.49
  8.9 0.7 broadcast_multiply_fusion.1
  9.7 0.0 all-gather.3.cloned.1.call-update
  9.7 0.0 copy-start.7
  9.7 0.0 copy-start.9
  9.7 0.0 all-reduce.11.cloned.1.call-start
  9.8 38.7 %all-gather.3.cloned.1.call-done = bf16[3,16,1,128,128]{3,4,1,0,2:T(8,128)(2,1)} async-done(((bf16[3,1,1,128,128]{3,4,1,0,2:T(8,128)(2,1)}), bf16[3,16,1,128,128]{3,4,1,0,2:T(8,128)(2,1)}) %all-gather.3.cloned.1.call-update) | async-done | bytes 1572880 | tf_op jit(solution)/shard_map/all_gather | solution.py:18
  48.5 7.5 fusion.10
  55.9 0.0 all-reduce.11.cloned.1.call-update
  56.0 0.0 all-gather.5.cloned.1.call-start
  56.0 0.2 copy.51
  56.2 0.8 broadcast_multiply_fusion
  57.0 0.0 all-gather.5.cloned.1.call-update
  57.0 0.0 all-reduce.15.cloned.1.call-start
  57.1 0.6 dynamic-slice
  57.7 0.0 copy-done.10
  57.7 166.9 %all-reduce.11.cloned.1.call-done = f32[16,1,3,128,128]{3,4,0,2,1:T(8,128)} async-done(((f32[16,1,3,128,128]{3,4,0,2,1:T(8,128)}), f32[16,1,3,128,128]{3,4,0,2,1:T(8,128)}) %all-reduce.11.cloned.1.call-update) | async-done | bytes 3145744
  224.6 1.6 constant_dynamic-slice_fusion.1
  226.2 0.1 copy.50
  226.4 0.7 fusion.37
  227.1 0.6 gather_fusion
  227.7 0.9 fusion.27
  228.6 2.2 fusion.21
  230.8 0.0 all-reduce.15.cloned.1.call-update
  230.8 0.0 all-reduce.13.cloned.1.call-start
  230.9 32.3 %all-gather.5.cloned.1.call-done = bf16[8,16,1,128,128]{3,4,1,0,2:T(8,128)(2,1)} async-done(((bf16[8,1,1,128,128]{3,4,1,0,2:T(8,128)(2,1)}), bf16[8,16,1,128,128]{3,4,1,0,2:T(8,128)(2,1)}) %all-gather.5.cloned.1.call-update) | async-done | bytes 4194320 | tf_op jit(solution)/shard_map/all_gather | solution.py:18
  263.2 13.6 %fusion.5 = f32[16,1,8,128,128]{3,4,0,2,1:T(8,128)} fusion(bf16[1,16,16,1,128,128]{5,4,3,2,1,0:T(8,128)(2,1)} %param.9, bf16[8,16,1,128,128]{3,4,1,0,2:T(8,128)(2,1)} %all-gather.5.cloned.1.call-done), kind=kOutput, calls=%fused_computation.7 | convolution fusion | flops 8589934592 | bytes 20971520 | tf_op jit(solution)/shard_map/aibjxy,kbjyz->iakxz/dot_general | solution.py:15
  276.8 111.3 %all-reduce.15.cloned.1.call-done = (f32[3,128,128]{2,1,0:T(8,128)}, f32[8,128,128]{2,1,0:T(8,128)}) async-done(((f32[3,128,128]{2,1,0:T(8,128)}, f32[8,128,128]{2,1,0:T(8,128)}), (f32[3,128,128]{2,1,0:T(8,128)}, f32[8,128,128]{2,1,0:T(8,128)})) %all-reduce.15.cloned.1.call-update) | async-done | bytes 720912 | tf_op jit(solution)/shard_map/psum | solution.py:10
  388.1 0.0 all-reduce.13.cloned.1.call-update
  388.1 0.0 copy-start.1
  388.1 0.0 all-reduce.9.cloned.1.call-start
  388.2 224.8 %all-reduce.13.cloned.1.call-done = (f32[3,128,128]{2,1,0:T(8,128)}, f32[16,1,8,128,128]{3,4,0,2,1:T(8,128)}, f32[8,128,128]{2,1,0:T(8,128)}) async-done(((f32[3,128,128]{2,1,0:T(8,128)}, f32[16,1,8,128,128]{3,4,0,2,1:T(8,128)}, f32[8,128,128]{2,1,0:T(8,128)}), (f32[3,128,128]{2,1,0:T(8,128)}, f32[16,1,8,128,128]{3,4,0,2,1:T(8,128)}, f32[8,128,128]{2,1,0:T(8,128)})) %all-reduce.13.cloned.1.call-update) | async-done | bytes 9109520 | tf_op jit(solution)/shard_map/psum | solution.py:11
  613.0 1.0 sub.12
  614.0 0.0 copy-start.2
  614.1 0.6 gather_fusion.1
  614.6 1.7 constant_dynamic-slice_fusion
  616.4 0.2 copy.52
  616.6 0.3 fusion.17
  616.9 0.0 copy-start.4
  616.9 1.0 fusion.19
  617.9 0.0 all-reduce.9.cloned.1.call-update
  617.9 1.5 convolution_subtract_fusion
  619.4 0.0 copy-start.3
  619.5 251.0 %all-reduce.9.cloned.1.call-done = f32[8,128,128]{2,1,0:T(8,128)} async-done(((f32[8,128,128]{2,1,0:T(8,128)}), f32[8,128,128]{2,1,0:T(8,128)}) %all-reduce.9.cloned.1.call-update) | async-done | bytes 524304 | tf_op jit(solution)/shard_map/psum | solution.py:72
  870.4 2.3 fusion.16
  (20 shorter events, 0.1 us)
Async XLA Ops:
  7.2 609.4 %copy-start = (bf16[8,128,128]{2,1,0:T(8,128)(2,1)S(1)}, bf16[8,128,128]{2,1,0:T(8,128)(2,1)}, u32[]{:S(2)}) copy-start(bf16[8,128,128]{2,1,0:T(8,128)(2,1)} %param.16) | copy-start | bytes 786436
  7.2 41.3 %all-gather.3.cloned.1.call-start = ((), (), s32[]{:S(2)}) async-start(), calls=%async_computation | async-start | bytes 1671168 | tf_op jit(solution)/shard_map/all_gather | solution.py:18
  9.7 46.3 %copy-start.7 = (bf16[8,1,1,128,128]{4,3,2,1,0:T(8,128)(2,1)S(1)}, bf16[8,1,1,128,128]{4,3,2,1,0:T(8,128)(2,1)}, u32[]{:S(2)}) copy-start(bf16[8,1,1,128,128]{4,3,2,1,0:T(8,128)(2,1)} %param.13) | copy-start | bytes 786436
  9.7 46.5 %copy-start.9 = (s32[8,1,1]{0,2,1:T(1,128)S(1)}, s32[8,1,1]{0,2,1:T(1,128)}, u32[]{:S(2)}) copy-start(s32[8,1,1]{0,2,1:T(1,128)} %param.14) | copy-start | bytes 100
  9.7 214.9 %all-reduce.11.cloned.1.call-start = ((), (), s32[]{:S(2)}) async-start(), calls=%async_computation.3 | async-start | bytes 6291456
  55.9 1.2 copy-start.11
  55.9 1.8 copy-start.10
  55.9 171.8 %copy-start.5 = (bf16[3,1,1,128,128]{3,4,1,0,2:T(8,128)(2,1)S(1)}, bf16[3,1,1,128,128]{3,4,1,0,2:T(8,128)(2,1)}, u32[]{:S(2)}) copy-start(bf16[3,1,1,128,128]{3,4,1,0,2:T(8,128)(2,1)} %broadcast_multiply_fusion.1) | copy-start | bytes 294916
  56.0 207.2 %all-gather.5.cloned.1.call-start = ((), (), s32[]{:S(2)}) async-start(), calls=%async_computation.1 | async-start | bytes 4456448 | tf_op jit(solution)/shard_map/all_gather | solution.py:18
  57.0 331.1 %all-reduce.15.cloned.1.call-start = ((), (), s32[]{:S(2)}) async-start(), calls=%async_computation.5 | async-start | bytes 1441792 | tf_op jit(solution)/shard_map/psum | solution.py:10
  230.8 382.2 %all-reduce.13.cloned.1.call-start = ((), (), s32[]{:S(2)}) async-start(), calls=%async_computation.4 | async-start | bytes 18219008 | tf_op jit(solution)/shard_map/psum | solution.py:11
  388.1 224.9 %copy-start.8 = (f32[3,128,128]{2,1,0:T(8,128)S(1)}, f32[3,128,128]{2,1,0:T(8,128)}, u32[]{:S(2)}) copy-start(f32[3,128,128]{2,1,0:T(8,128)} %param.12) | copy-start | bytes 589828
  388.1 228.8 %copy-start.1 = (bf16[8,1,1,128,128]{3,4,1,0,2:T(8,128)(2,1)S(1)}, bf16[8,1,1,128,128]{3,4,1,0,2:T(8,128)(2,1)}, u32[]{:S(2)}) copy-start(bf16[8,1,1,128,128]{3,4,1,0,2:T(8,128)(2,1)} %broadcast_multiply_fusion) | copy-start | bytes 786436
  388.1 482.3 %all-reduce.9.cloned.1.call-start = ((), (), s32[]{:S(2)}) async-start(), calls=%async_computation.2 | async-start | bytes 1048576 | tf_op jit(solution)/shard_map/psum | solution.py:72
  613.0 257.4 %copy-start.6 = (f32[8,128,128]{2,1,0:T(8,128)S(1)}, f32[8,128,128]{2,1,0:T(8,128)}, u32[]{:S(2)}) copy-start(f32[8,128,128]{2,1,0:T(8,128)} %param.17) | copy-start | bytes 1572868
  614.0 258.7 %copy-start.2 = (f32[3,128,128]{2,1,0:T(8,128)}, f32[3,128,128]{2,1,0:T(8,128)S(1)}, u32[]{:S(2)}) copy-start(f32[3,128,128]{2,1,0:T(8,128)S(1)} %sub.12) | copy-start | bytes 589828
  616.9 255.8 %copy-start.4 = (bf16[8,128,128]{2,1,0:T(8,128)(2,1)}, bf16[8,128,128]{2,1,0:T(8,128)(2,1)S(1)}, u32[]{:S(2)}) copy-start(bf16[8,128,128]{2,1,0:T(8,128)(2,1)S(1)} %fusion.17) | copy-start | bytes 786436
  619.4 253.3 %copy-start.3 = (f32[8,128,128]{2,1,0:T(8,128)}, f32[8,128,128]{2,1,0:T(8,128)S(1)}, u32[]{:S(2)}) copy-start(f32[8,128,128]{2,1,0:T(8,128)S(1)} %convolution_subtract_fusion) | copy-start | bytes 1572868
Sparse Core Ops, SparseCore 0:
  10.4 38.0 all-gather.2
  56.1 168.5 all-reduce.10
  227.0 36.0 all-gather.4
  266.3 121.7 all-reduce.14
  390.9 222.1 all-reduce.12
  618.9 251.4 all-reduce.8
